TPU v7x, 32 devices: a whole 2x2x4 slice. The times are simulated.
32 devices in a mesh: grid: 8 (over z, y), tile: 4 (over x, core).
Axes of the slice: x: 2, y: 2, z: 4, core: 2. Of those that a mesh axis runs over, the one named last changes fastest.
Arguments:
- point_values: bfloat16 [256, 16384], P('grid', 'tile'), may hold values from -1.75 to 1.75
- sig_blocks: int32 [8, 16], P('grid'), may hold values from 0 to 31, as said below
- density: bfloat16 [16384, 16384], P('grid', 'tile'), may hold values from -0.0625 to 0.0625
- coulomb_core: bfloat16 [512, 512], replicated, may hold values from -0.25 to 0.25
- screen_mask: int32 [32, 32], replicated, may hold values 0 or 1
- ao_centers: float32 [3, 16384], replicated, may hold values from -1 to 1
- ao_widths: float32 [16384], replicated, may hold values from 0.25 to 1
- point_coords: float32 [3, 256], P(None, 'grid'), may hold values from -1 to 1
- lmo_coeffs: bfloat16 [16384, 1024], P('tile'), may hold values from -0.0625 to 0.0625
- domain_blocks: int32 [4, 16], replicated, may hold values from 0 to 31, as said below
Outputs:
- half: bfloat16 [1024, 16384], P('tile', 'grid')
Inputs may be any that keep to these rules, and one draw needn't show every extreme that they name: `sig_blocks`: each batch names 16 different AO blocks. `domain_blocks`: each strip's 16 blocks are different, and every AO block lies in the domain of some strip.
All inputs are finite; a program needn't handle non-finite values.
Results may differ from a plain program's by a relative error of at most 0.02.
Values may be sent and summed in bfloat16 or wider, within the bound.
A program may use at most 128 MiB of HBM per device.

v0:
```python
import jax
import jax.numpy as jnp
from jax import lax
from jax.sharding import PartitionSpec as P

highest = lax.Precision.HIGHEST


def kernel_weights(ao_centers, ao_widths, point_coords):
    offsets = ao_centers[:, None, :] - point_coords[:, :, None]
    return 1.0 / jnp.sqrt(jnp.sum(offsets * offsets, axis=0) + ao_widths[None, :])


def spread_mask(flag_rows, batch_points, block_size):
    batches, block_count = flag_rows.shape
    expanded = jnp.broadcast_to(
        flag_rows[:, None, :, None], (batches, batch_points, block_count, block_size)
    )
    return expanded.reshape(batches * batch_points, block_count * block_size)


def shards(
    point_values,
    sig_blocks,
    density,
    coulomb_core,
    screen_mask,
    ao_centers,
    ao_widths,
    point_coords,
    lmo_coeffs,
    domain_blocks,
):
    grid_count = lax.axis_size("grid")
    panel_index = lax.axis_index("tile")
    batches = sig_blocks.shape[0]
    own_rows, own_cols = density.shape
    points = point_values.shape[0]
    batch_points = points // batches
    block_size = coulomb_core.shape[0]
    total_aos = ao_widths.shape[0]
    all_blocks = total_aos // block_size
    col_blocks = own_cols // block_size
    row_blocks = own_rows // block_size
    block_ids = jnp.arange(all_blocks, dtype=jnp.int32)
    named_blocks = jnp.any(sig_blocks[:, :, None] == block_ids[None, None, :], axis=1).astype(
        jnp.float32
    )
    first_col = panel_index * col_blocks
    named_cols = lax.dynamic_slice_in_dim(named_blocks, first_col, col_blocks, 1)
    col_mask = spread_mask(named_cols, batch_points, block_size)
    masked_local = point_values * col_mask.astype(jnp.bfloat16)
    dest_named = jnp.max(named_blocks.reshape(batches, grid_count, row_blocks), axis=2)
    outgoing = masked_local.reshape(batches, batch_points, 1, own_cols) * dest_named[
        :, None, :, None
    ].astype(jnp.bfloat16)
    product = jnp.einsum(
        "bpgc,rc->bpgr",
        lax.all_to_all(outgoing, "grid", split_axis=2, concat_axis=2, tiled=True),
        density,
        preferred_element_type=jnp.float32,
    )
    arrivals = lax.all_to_all(
        product.astype(jnp.bfloat16), "grid", split_axis=2, concat_axis=2, tiled=True
    )
    row_mask = spread_mask(named_blocks, batch_points, block_size)
    partial_term = arrivals.reshape(points, total_aos).astype(jnp.float32) * row_mask
    coefficient = kernel_weights(ao_centers, ao_widths, point_coords)
    core_float = coulomb_core.astype(jnp.float32)
    screen_float = screen_mask.astype(jnp.float32)
    density_term = lax.psum(partial_term.astype(jnp.bfloat16), "tile").astype(jnp.float32)
    weighted = (coefficient * density_term).reshape(points, all_blocks, block_size)
    screen_rows = lax.dynamic_slice_in_dim(screen_float, first_col, col_blocks, 0)
    screened = jnp.einsum("kj,pja->pka", screen_rows, weighted, precision=highest)
    kernel_part = jnp.einsum(
        "ab,pkb->pka", core_float, screened, preferred_element_type=jnp.float32
    ).reshape(points, own_cols)
    coeff_cols = lax.dynamic_slice_in_dim(coefficient, panel_index * own_cols, own_cols, 1)
    potential = (coeff_cols * kernel_part * col_mask).astype(jnp.bfloat16)
    potential_out = jnp.broadcast_to(
        potential.reshape(batches, batch_points, 1, own_cols),
        (batches, batch_points, grid_count, own_cols),
    )
    whole_points = lax.all_gather(masked_local, "tile", axis=1, tiled=True)
    row_values, col_values = (
        lax.all_to_all(
            whole_points.reshape(batches, batch_points, grid_count, own_rows),
            "grid",
            split_axis=2,
            concat_axis=2,
            tiled=True,
        ),
        lax.all_to_all(potential_out, "grid", split_axis=2, concat_axis=2, tiled=True),
    )
    exch_tile = jnp.einsum(
        "bpgr,bpgc->rc", row_values, col_values, preferred_element_type=jnp.float32
    ).astype(jnp.bfloat16)
    number_of_slabs = domain_blocks.shape[0]
    localized_orbital_total = lmo_coeffs.shape[1]
    strip_width = localized_orbital_total // number_of_slabs
    local_ids = first_col + jnp.arange(col_blocks, dtype=jnp.int32)
    in_domain = jnp.any(domain_blocks[:, :, None] == local_ids[None, None, :], axis=1)
    domain_flags = jnp.transpose(in_domain)
    domain_mask = jnp.broadcast_to(
        domain_flags[:, None, :, None], (col_blocks, block_size, number_of_slabs, strip_width)
    ).reshape(own_cols, localized_orbital_total)
    region_expansion_factor = lmo_coeffs * domain_mask.astype(jnp.bfloat16)
    return lax.psum_scatter(
        lax.dot_general(
            region_expansion_factor,
            exch_tile,
            (((0,), (1,)), ((), ())),
            preferred_element_type=jnp.float32,
        ).astype(jnp.bfloat16),
        "tile",
        scatter_dimension=0,
        tiled=True,
    )


def solution(mesh):
    in_specs = (
        P("grid", "tile"),
        P("grid", None),
        P("grid", "tile"),
        P(),
        P(),
        P(),
        P(),
        P(None, "grid"),
        P("tile", None),
        P(),
    )
    out_specs = P("tile", "grid")
    return jax.shard_map(shards, mesh=mesh, in_specs=in_specs, out_specs=out_specs, check_vma=False)
```

profile of v0, /device:TPU:0, one launch (start us, length us, event | category | flops | bytes accessed | tf_op | source)
XLA Modules:
  0.0 288.2 jit_solution(9041671634119760462)
XLA Ops:
  6.5 0.8 fusion.26
  7.6 0.1 reduce_max.9
  7.7 1.0 broadcast_multiply_fusion.1
  8.7 0.2 broadcast_multiply_fusion
  8.9 55.3 %all_to_all.20 = bf16[1,32,8,4096]{3,1,0,2:T(8,128)(2,1)S(1)} all-to-all(bf16[1,32,8,4096]{3,1,0,2:T(8,128)(2,1)S(1)} %broadcast_multiply_fusion), channel_id=1, replica_groups=mesh['grid'=8,'tile'=4] {'grid'}, dimensions={2} | all-to-all | bytes 4194304 | tf_op jit(solution)/shard_map/all_to_all | solution.py:59
  64.3 9.6 %fusion.11 = bf16[1,32,8,2048]{3,2,1,0:T(8,128)(2,1)} fusion(bf16[2048,4096]{1,0:T(8,128)(2,1)} %param.12, bf16[1,32,8,4096]{3,1,0,2:T(8,128)(2,1)S(1)} %all_to_all.20), kind=kOutput, calls=%fused_computation.9 | convolution fusion | flops 4295491584 | bytes 19922944 | tf_op jit(solution)/shard_map/bpgc,rc->bpgr/dot_general | solution.py:57
  73.8 2.8 copy.25
  76.6 3.6 %all-to-all-start.2 = ((bf16[1,32,8,2048]{3,1,0,2:T(8,128)(2,1)}), bf16[1,32,8,2048]{3,1,0,2:T(8,128)(2,1)S(1)}, u32[]{:S(2)}, u32[]{:S(2)}) async-start(bf16[1,32,8,2048]{3,1,0,2:T(8,128)(2,1)} %copy.25), calls=%async_computation.2 | async-start | bytes 2097152 | tf_op jit(solution)/shard_map/all_to_all | solution.py:63
  80.2 0.7 all-gather.2.cloned.1.call-update
  81.1 24.7 %all-to-all-done.2 = bf16[1,32,8,2048]{3,1,0,2:T(8,128)(2,1)S(1)} async-done(((bf16[1,32,8,2048]{3,1,0,2:T(8,128)(2,1)}), bf16[1,32,8,2048]{3,1,0,2:T(8,128)(2,1)S(1)}, u32[]{:S(2)}, u32[]{:S(2)}) %all-to-all-start.2) | async-done | bytes 1048608 | tf_op jit(solution)/shard_map/all_to_all | solution.py:63
  105.8 0.2 copy.31
  106.0 1.1 multiply_convert_fusion
  107.2 0.8 multiply_reduce_fusion
  108.0 1.8 copy.30
  109.9 1.6 copy.22
  111.5 4.2 %all-to-all-start = ((bf16[1,32,8,2048]{3,1,0,2:T(8,128)(2,1)}), bf16[1,32,8,2048]{3,1,0,2:T(8,128)(2,1)}, u32[]{:S(2)}, u32[]{:S(2)}) async-start(bf16[1,32,8,2048]{3,1,0,2:T(8,128)(2,1)} %copy.22), calls=%async_computation | async-start | bytes 2097152 | tf_op jit(solution)/shard_map/all_to_all | solution.py:86
  115.7 26.8 %all-reduce.2.cloned.1.call-done = bf16[32,16384]{1,0:T(8,128)(2,1)} async-done(((bf16[32,16384]{1,0:T(8,128)(2,1)}), bf16[32,16384]{1,0:T(8,128)(2,1)}) %all-reduce.2.cloned.1.call-update) | async-done | bytes 1048592 | tf_op jit(solution)/shard_map/psum | solution.py:71
  142.5 1.5 convert_multiply_fusion
  144.0 1.2 copy.33
  145.2 1.9 convolution_bitcast_fusion
  147.1 0.3 fusion.24
  147.5 0.3 copy.34
  147.9 1.6 broadcast_in_dim.49
  149.5 5.9 %all-to-all-start.3 = ((bf16[1,32,8,4096]{3,1,0,2:T(8,128)(2,1)}), bf16[1,32,8,4096]{3,1,0,2:T(8,128)(2,1)S(1)}, u32[]{:S(2)}, u32[]{:S(2)}) async-start(bf16[1,32,8,4096]{3,1,0,2:T(8,128)(2,1)} %broadcast_in_dim.49), calls=%async_computation.3 | async-start | bytes 4194304 | tf_op jit(solution)/shard_map/all_to_all | solution.py:93
  155.4 0.2 reduce-scatter.2.cloned.1.call-start
  155.7 0.2 compare_reduce_fusion
  156.0 2.2 broadcast_in_dim.18
  158.2 4.0 %copy.28 = pred[512,8,4,256]{3,1,2,0:T(8,128)(4,1)} copy(pred[512,8,4,256]{3,2,1,0:T(4,128)(4,1)S(1)} %bitcast.72) | data formatting | bytes 8388608
  162.3 40.5 %all-to-all-done.3 = bf16[1,32,8,4096]{3,1,0,2:T(8,128)(2,1)S(1)} async-done(((bf16[1,32,8,4096]{3,1,0,2:T(8,128)(2,1)}), bf16[1,32,8,4096]{3,1,0,2:T(8,128)(2,1)S(1)}, u32[]{:S(2)}, u32[]{:S(2)}) %all-to-all-start.3) | async-done | bytes 2097184 | tf_op jit(solution)/shard_map/all_to_all | solution.py:93
  202.8 10.0 %bitcast_convert_fusion.clone.7 = bf16[2048,4096]{1,0:T(8,128)(2,1)} fusion(bf16[1,32,8,4096]{3,1,0,2:T(8,128)(2,1)S(1)} %all-to-all-done.3, bf16[1,32,8,2048]{3,1,0,2:T(8,128)(2,1)} %all-to-all-done), kind=kOutput, calls=%fused_computation.clone.clone.clone.clone.clone.2 | convolution fusion | flops 4303355904 | bytes 19922944 | tf_op jit(solution)/shard_map/bpgr,bpgc->rc/dot_general | solution.py:95
  212.8 25.2 %fusion.5 = bf16[1024,2048]{1,0:T(8,128)(2,1)} fusion(pred[4096,1024]{1,0:T(8,128)(4,1)} %bitcast.77, bf16[4096,1024]{1,0:T(8,128)(2,1)} %param.18, bf16[2048,4096]{1,0:T(8,128)(2,1)} %bitcast_convert_fusion.clone.7), kind=kOutput, calls=%fused_computation.7 | convolution fusion | flops 17186160640 | bytes 33554432 | tf_op jit(solution)/shard_map/dot_general | solution.py:109
  237.9 43.7 %reduce-scatter.2.cloned.1.call-done = bf16[256,2048]{1,0:T(8,128)(2,1)} async-done(((bf16[1024,2048]{1,0:T(8,128)(2,1)}), bf16[256,2048]{1,0:T(8,128)(2,1)}) %reduce-scatter.2.cloned.1.call-update) | async-done | bytes 1048592 | tf_op jit(solution)/shard_map/reduce_scatter | solution.py:108
  (31 shorter events, 0.7 us)
Async XLA Ops:
  6.5 140.6 %copy-start = (bf16[512,512]{1,0:T(8,128)(2,1)S(1)}, bf16[512,512]{1,0:T(8,128)(2,1)}, u32[]{:S(2)}) copy-start(bf16[512,512]{1,0:T(8,128)(2,1)} %param.13) | copy-start | bytes 1572868
  8.7 55.6 %copy-start.2 = (bf16[32,4096]{1,0:T(8,128)(2,1)}, bf16[32,4096]{1,0:T(8,128)(2,1)S(1)}, u32[]{:S(2)}) copy-start(bf16[32,4096]{1,0:T(8,128)(2,1)S(1)} %broadcast_multiply_fusion.1) | copy-start | bytes 786436
  76.6 29.2 %all-to-all-start.2 = ((bf16[1,32,8,2048]{3,1,0,2:T(8,128)(2,1)}), bf16[1,32,8,2048]{3,1,0,2:T(8,128)(2,1)S(1)}, u32[]{:S(2)}, u32[]{:S(2)}) async-start(bf16[1,32,8,2048]{3,1,0,2:T(8,128)(2,1)} %copy.25), calls=%async_computation.2 | async-start | bytes 2097152 | tf_op jit(solution)/shard_map/all_to_all | solution.py:63
  80.2 27.8 %all-gather.2.cloned.1.call-start = ((), (), s32[]{:S(2)}) async-start(), calls=%async_computation.5 | async-start | bytes 1310720 | tf_op jit(solution)/shard_map/all_gather | solution.py:84
  80.9 61.6 %all-reduce.2.cloned.1.call-start = ((), (), s32[]{:S(2)}) async-start(), calls=%async_computation.6 | async-start | bytes 2097152 | tf_op jit(solution)/shard_map/psum | solution.py:71
  106.0 1.2 copy-start.3
  106.0 1.2 copy-start.6
  109.8 32.6 %copy-start.4 = (f32[16384]{0:T(1024)S(1)}, f32[16384]{0:T(1024)}, u32[]{:S(2)}) copy-start(f32[16384]{0:T(1024)} %param.16) | copy-start | bytes 196612
  111.5 36.4 %all-to-all-start = ((bf16[1,32,8,2048]{3,1,0,2:T(8,128)(2,1)}), bf16[1,32,8,2048]{3,1,0,2:T(8,128)(2,1)}, u32[]{:S(2)}, u32[]{:S(2)}) async-start(bf16[1,32,8,2048]{3,1,0,2:T(8,128)(2,1)} %copy.22), calls=%async_computation | async-start | bytes 2097152 | tf_op jit(solution)/shard_map/all_to_all | solution.py:86
  149.5 6.2 %copy-start.5 = (s32[4,16]{1,0:T(4,128)S(1)}, s32[4,16]{1,0:T(4,128)}, u32[]{:S(2)}) copy-start(s32[4,16]{1,0:T(4,128)} %param.19) | copy-start | bytes 772
  149.5 53.3 %all-to-all-start.3 = ((bf16[1,32,8,4096]{3,1,0,2:T(8,128)(2,1)}), bf16[1,32,8,4096]{3,1,0,2:T(8,128)(2,1)S(1)}, u32[]{:S(2)}, u32[]{:S(2)}) async-start(bf16[1,32,8,4096]{3,1,0,2:T(8,128)(2,1)} %broadcast_in_dim.49), calls=%async_computation.3 | async-start | bytes 4194304 | tf_op jit(solution)/shard_map/all_to_all | solution.py:93
  155.4 126.2 %reduce-scatter.2.cloned.1.call-start = ((), (), s32[]{:S(2)}) async-start(), calls=%async_computation.7 | async-start | bytes 5242880 | tf_op jit(solution)/shard_map/reduce_scatter | solution.py:108
  237.9 43.7 %copy-start.1 = (bf16[512,512]{1,0:T(8,128)(2,1)S(1)}, bf16[512,512]{1,0:T(8,128)(2,1)}, u32[]{:S(2)}) copy-start(bf16[512,512]{1,0:T(8,128)(2,1)} %param.13) | copy-start | bytes 1572868
Sparse Core Ops, SparseCore 0:
  82.6 18.0 all-gather.1
  107.3 35.1 all-reduce.1
  238.1 43.5 reduce-scatter.1
where the time goes:
time: 289 us; the launch traced here: 288 us
  waiting for transfers between devices  136 us (47%)
  blocking collectives  55.3 us (19%)
  matrix products  46.9 us (16%)
  local copies, waits for them, and re-layouts  16.3 us (6%)
  starting transfers between devices  14 us (5%)
  between operations  13.3 us (5%)
  other arithmetic  5.85 us (2%)
    all_to_all x1, blocking collectives, shards(): lax.all_to_all(outgoing, 'grid', split_axis=2, concat_axis=2, tiled=True)  55.3 us
    reduce_scatter x1, waiting for transfers between devices, shards(): lax.psum_scatter(lax.dot_general(region_expansion_factor, exch_tile, (((0...  43.7 us
    all_to_all x1, waiting for transfers between devices, shards(): lax.all_to_all(potential_out, 'grid', split_axis=2, concat_axis=2, tiled=...  40.5 us
    psum x1, waiting for transfers between devices, shards(): lax.psum(partial_term.astype(jnp.bfloat16), 'tile').astype(jnp.float32)  26.8 us
    dot_general x1, matrix products, shards(): lax.dot_general(region_expansion_factor, exch_tile, (((0,), (1,)), ((), (...  25.2 us
    all_to_all x1, waiting for transfers between devices, shards(): lax.all_to_all(product.astype(jnp.bfloat16), 'grid', split_axis=2, concat...  24.7 us
    dot_general x1, matrix products, shards(): jnp.einsum('bpgr,bpgc->rc', row_values, col_values, preferred_element_typ...  9.96 us
    dot_general x1, matrix products, shards(): jnp.einsum('bpgc,rc->bpgr', lax.all_to_all(outgoing, 'grid', split_axis=2...  9.56 us
  transfers between devices with their start and end apart: 6, of which 4 were waited for; matrix products, arithmetic and copies ran while one was open for 6% of the time, Pallas kernels for 0%

commit v1 on v0

--- a/solution.py
+++ b/solution.py
@@ -4,6 +4,29 @@
 from jax.sharding import PartitionSpec as P
 
 highest = lax.Precision.HIGHEST
+
+
+def split_up(value, dim, peers):
+    before, after = (value.shape[:dim], value.shape[dim + 1 :])
+    return jnp.moveaxis(value.reshape(*before, peers, -1, *after), dim, 0)
+
+
+def laid_out(tiles, dim):
+    tiles = jnp.moveaxis(tiles, 0, dim)
+    dims = tiles.shape
+    return tiles.reshape(*dims[:dim], dims[dim] * dims[dim + 1], *dims[dim + 2 :])
+
+
+def sent_to_each(x, axis, split_dim, concat_dim):
+    size, place = (lax.axis_size(axis), lax.axis_index(axis))
+    tiles = split_up(x, split_dim, size)
+    out = tiles
+    for lap in range(1, size):
+        target, source = ((place + lap) % size, (place - lap) % size)
+        sent = lax.dynamic_index_in_dim(tiles, target, 0)
+        other = lax.ppermute(sent, axis, [(i, (i + lap) % size) for i in range(size)])
+        out = lax.dynamic_update_slice_in_dim(out, other, source, axis=0)
+    return laid_out(out, concat_dim)
 
 
 def kernel_weights(ao_centers, ao_widths, point_coords):
@@ -60,9 +83,7 @@
         density,
         preferred_element_type=jnp.float32,
     )
-    arrivals = lax.all_to_all(
-        product.astype(jnp.bfloat16), "grid", split_axis=2, concat_axis=2, tiled=True
-    )
+    arrivals = sent_to_each(product.astype(jnp.bfloat16), "grid", 2, 2)
     row_mask = spread_mask(named_blocks, batch_points, block_size)
     partial_term = arrivals.reshape(points, total_aos).astype(jnp.float32) * row_mask
     coefficient = kernel_weights(ao_centers, ao_widths, point_coords)

time: 289 us -> 322 us (1.11)
  blocking collectives: 55.3 us -> 0 us
  waiting for transfers between devices: 136 us -> 186 us
  starting transfers between devices: 14 us -> 34.6 us
  local copies, waits for them, and re-layouts: 16.3 us -> 31.4 us
    all_to_all x1 -> x0, blocking collectives: 55.3 us -> none  [shards(): lax.all_to_all(outgoing, 'grid', split_axis=2, concat_axis=2, tiled=True)]
    ppermute x0 -> x7, waiting for transfers between devices: none -> 27.9 us  [sent_to_each(): lax.ppermute(sent, axis, [(i, (i + lap) % size) for i in range(size)])]
    all_to_all x1, waiting for transfers between devices: 24.7 us -> 48.2 us  [shards(): lax.all_to_all(outgoing, 'grid', split_axis=2, concat_axis=2, tiled=True)]
    ppermute x0 -> x7, starting transfers between devices: none -> 17.1 us  [sent_to_each(): lax.ppermute(sent, axis, [(i, (i + lap) % size) for i in range(size)])]
    dynamic_update_slice x0 -> x7, local copies, waits for them, and re-layouts: none -> 14.1 us  [sent_to_each(): out = lax.dynamic_update_slice_in_dim(out, other, source, axis=0)]
    all_to_all x1, starting transfers between devices: 3.59 us -> 7.31 us  [shards(): lax.all_to_all(outgoing, 'grid', split_axis=2, concat_axis=2, tiled=True)]
  transfers between devices with their start and end apart: 6 -> 13, of which waited for: 4 -> 6; matrix products, arithmetic and copies ran while one was open for 6% -> 10% of each run, Pallas kernels for 0% -> 0%
where the time goes in v1:
time: 322 us
  waiting for transfers between devices  186 us (58%)
  matrix products  48.9 us (15%)
  starting transfers between devices  34.6 us (11%)
  local copies, waits for them, and re-layouts  31.4 us (10%)
  between operations  13.7 us (4%)
  other arithmetic  7.39 us (2%)
    all_to_all x1, waiting for transfers between devices, shards(): lax.all_to_all(outgoing, 'grid', split_axis=2, concat_axis=2, tiled=True)  48.2 us
    reduce_scatter x1, waiting for transfers between devices, shards(): lax.psum_scatter(lax.dot_general(region_expansion_factor, exch_tile, (((0...  43.6 us
    all_to_all x1, waiting for transfers between devices, shards(): lax.all_to_all(potential_out, 'grid', split_axis=2, concat_axis=2, tiled=...  40.6 us
    ppermute x7, waiting for transfers between devices, sent_to_each(): lax.ppermute(sent, axis, [(i, (i + lap) % size) for i in range(size)])  27.9 us
    psum x1, waiting for transfers between devices, shards(): lax.psum(partial_term.astype(jnp.bfloat16), 'tile').astype(jnp.float32)  25.5 us
    dot_general x1, matrix products, shards(): lax.dot_general(region_expansion_factor, exch_tile, (((0,), (1,)), ((), (...  25.2 us
    ppermute x7, starting transfers between devices, sent_to_each(): lax.ppermute(sent, axis, [(i, (i + lap) % size) for i in range(size)])  17.1 us
    dynamic_update_slice x7, local copies, waits for them, and re-layouts, sent_to_each(): out = lax.dynamic_update_slice_in_dim(out, other, source, axis=0)  14.1 us
  transfers between devices with their start and end apart: 13, of which 6 were waited for; matrix products, arithmetic and copies ran while one was open for 10% of the time, Pallas kernels for 0%

profile of v1, /device:TPU:0, one launch (start us, length us, event | category | flops | bytes accessed | tf_op | source)
XLA Modules:
  0.0 321.8 jit_solution(17234974939090938909)
XLA Ops:
  8.7 1.5 broadcast_multiply_fusion
  10.2 7.3 %all-to-all-start.1 = ((bf16[1,32,8,4096]{3,1,0,2:T(8,128)(2,1)}), bf16[1,32,8,4096]{3,1,0,2:T(8,128)(2,1)}, u32[]{:S(2)}, u32[]{:S(2)}) async-start(bf16[1,32,8,4096]{3,1,0,2:T(8,128)(2,1)} %broadcast_multiply_fusion), calls=%async_computation.1 | async-start | bytes 4194304 | tf_op jit(solution)/shard_map/all_to_all | solution.py:82
  17.7 48.2 %all-to-all-done.1 = bf16[1,32,8,4096]{3,1,0,2:T(8,128)(2,1)} async-done(((bf16[1,32,8,4096]{3,1,0,2:T(8,128)(2,1)}), bf16[1,32,8,4096]{3,1,0,2:T(8,128)(2,1)}, u32[]{:S(2)}, u32[]{:S(2)}) %all-to-all-start.1) | async-done | bytes 2097184 | tf_op jit(solution)/shard_map/all_to_all | solution.py:82
  65.9 11.5 %fusion.8 = bf16[32,8,2048]{2,1,0:T(8,128)(2,1)S(1)} fusion(bf16[2048,4096]{1,0:T(8,128)(2,1)} %param.12, bf16[1,32,8,4096]{3,1,0,2:T(8,128)(2,1)} %all-to-all-done.1), kind=kOutput, calls=%fused_computation.8 | convolution fusion | flops 4295491584 | bytes 19922944 | tf_op jit(solution)/shard_map/bpgc,rc->bpgr/dot_general | solution.py:80
  77.4 2.9 dynamic-slice_bitcast_fusion
  80.3 1.5 collective-permute-start
  81.9 3.3 %collective-permute-start.6 = (bf16[1,1,32,1,2048]{4,0,2,3,1:T(2,128)(2,1)}, bf16[1,1,32,1,2048]{4,0,2,3,1:T(2,128)(2,1)S(1)}, u32[]{:S(2)}, u32[]{:S(2)}) collective-permute-start(bf16[1,1,32,1,2048]{4,0,2,3,1:T(2,128)(2,1)} %get-tuple-element.7), channel_id=1, source_target_pairs={{0,28},{4,0},{8,4},{12,8},{16,12},{20,16},{24,20},{28,24},{1,29},{... | collective-permute-start | bytes 393224 | tf_op jit(solution)/shard_map/ppermute | solution.py:27
  85.2 2.0 collective-permute-start.5
  87.3 4.0 %collective-permute-done.1 = bf16[1,1,32,1,2048]{4,0,2,3,1:T(2,128)(2,1)S(1)} collective-permute-done((bf16[1,1,32,1,2048]{4,0,2,3,1:T(2,128)(2,1)S(1)}, bf16[1,1,32,1,2048]{4,0,2,3,1:T(2,128)(2,1)S(1)}, u32[]{:S(2)}, u32[]{:S(2)}) %collective-permute-start.1) | collective-permute-done | bytes 131104 | tf_op jit(solution)/shard_map/ppermute | solution.py:27
  91.2 10.3 %collective-permute-start.3 = (bf16[1,1,32,1,2048]{4,0,2,3,1:T(2,128)(2,1)}, bf16[1,1,32,1,2048]{4,0,2,3,1:T(2,128)(2,1)S(1)}, u32[]{:S(2)}, u32[]{:S(2)}) collective-permute-start(bf16[1,1,32,1,2048]{4,0,2,3,1:T(2,128)(2,1)} %get-tuple-element.10), channel_id=1, source_target_pairs={{0,16},{4,20},{8,24},{12,28},{16,0},{20,4},{24,8},{28,12},{1,17},{... | collective-permute-start | bytes 393224 | tf_op jit(solution)/shard_map/ppermute | solution.py:27
  101.6 2.0 dynamic_update_slice.21
  103.7 2.0 dynamic_update_slice.22
  105.7 23.9 %collective-permute-done.2 = bf16[1,1,32,1,2048]{4,0,2,3,1:T(2,128)(2,1)S(1)} collective-permute-done((bf16[1,1,32,1,2048]{4,0,2,3,1:T(2,128)(2,1)}, bf16[1,1,32,1,2048]{4,0,2,3,1:T(2,128)(2,1)S(1)}, u32[]{:S(2)}, u32[]{:S(2)}) %collective-permute-start.2) | collective-permute-done | bytes 131104 | tf_op jit(solution)/shard_map/ppermute | solution.py:27
  129.6 2.0 dynamic_update_slice.23
  131.6 2.0 dynamic_update_slice.24
  133.7 2.0 dynamic_update_slice.25
  135.7 2.0 dynamic_update_slice.26
  137.7 2.0 dynamic_update_slice.27
  143.3 1.8 copy.25
  145.1 1.6 copy.19
  146.6 4.2 %all-to-all-start = ((bf16[1,32,8,2048]{3,1,0,2:T(8,128)(2,1)}), bf16[1,32,8,2048]{3,1,0,2:T(8,128)(2,1)}, u32[]{:S(2)}, u32[]{:S(2)}) async-start(bf16[1,32,8,2048]{3,1,0,2:T(8,128)(2,1)} %copy.19), calls=%async_computation | async-start | bytes 2097152 | tf_op jit(solution)/shard_map/all_to_all | solution.py:107
  150.9 25.5 %all-reduce.2.cloned.1.call-done = bf16[32,16384]{1,0:T(8,128)(2,1)} async-done(((bf16[32,16384]{1,0:T(8,128)(2,1)}), bf16[32,16384]{1,0:T(8,128)(2,1)}) %all-reduce.2.cloned.1.call-update) | async-done | bytes 1048592 | tf_op jit(solution)/shard_map/psum | solution.py:92
  176.4 1.5 convert_multiply_fusion
  179.1 1.9 convolution_bitcast_fusion
  181.8 1.6 broadcast_in_dim.49
  183.3 5.6 %all-to-all-start.2 = ((bf16[1,32,8,4096]{3,1,0,2:T(8,128)(2,1)}), bf16[1,32,8,4096]{3,1,0,2:T(8,128)(2,1)S(1)}, u32[]{:S(2)}, u32[]{:S(2)}) async-start(bf16[1,32,8,4096]{3,1,0,2:T(8,128)(2,1)} %broadcast_in_dim.49), calls=%async_computation.2 | async-start | bytes 4194304 | tf_op jit(solution)/shard_map/all_to_all | solution.py:114
  189.6 2.2 broadcast_in_dim.18
  191.8 4.1 %copy.23 = pred[512,8,4,256]{3,1,2,0:T(8,128)(4,1)} copy(pred[512,8,4,256]{3,2,1,0:T(4,128)(4,1)S(1)} %bitcast.85) | data formatting | bytes 8388608
  195.9 40.6 %all-to-all-done.2 = bf16[1,32,8,4096]{3,1,0,2:T(8,128)(2,1)S(1)} async-done(((bf16[1,32,8,4096]{3,1,0,2:T(8,128)(2,1)}), bf16[1,32,8,4096]{3,1,0,2:T(8,128)(2,1)S(1)}, u32[]{:S(2)}, u32[]{:S(2)}) %all-to-all-start.2) | async-done | bytes 2097184 | tf_op jit(solution)/shard_map/all_to_all | solution.py:114
  236.5 10.0 %bitcast_convert_fusion.clone.7 = bf16[2048,4096]{1,0:T(8,128)(2,1)} fusion(bf16[1,32,8,4096]{3,1,0,2:T(8,128)(2,1)S(1)} %all-to-all-done.2, bf16[1,32,8,2048]{3,1,0,2:T(8,128)(2,1)} %all-to-all-done), kind=kOutput, calls=%fused_computation.clone.clone.clone.clone.clone.2 | convolution fusion | flops 4303355904 | bytes 19922944 | tf_op jit(solution)/shard_map/bpgr,bpgc->rc/dot_general | solution.py:116
  246.4 25.2 %fusion.5 = bf16[1024,2048]{1,0:T(8,128)(2,1)} fusion(pred[4096,1024]{1,0:T(8,128)(4,1)} %bitcast.91, bf16[4096,1024]{1,0:T(8,128)(2,1)} %param.18, bf16[2048,4096]{1,0:T(8,128)(2,1)} %bitcast_convert_fusion.clone.7), kind=kOutput, calls=%fused_computation.7 | convolution fusion | flops 17186160640 | bytes 33554432 | tf_op jit(solution)/shard_map/dot_general | solution.py:130
  271.6 43.6 %reduce-scatter.2.cloned.1.call-done = bf16[256,2048]{1,0:T(8,128)(2,1)} async-done(((bf16[1024,2048]{1,0:T(8,128)(2,1)}), bf16[256,2048]{1,0:T(8,128)(2,1)}) %reduce-scatter.2.cloned.1.call-update) | async-done | bytes 1048592 | tf_op jit(solution)/shard_map/reduce_scatter | solution.py:129
  (52 shorter events, 8.3 us)
Async XLA Ops:
  6.5 174.5 %copy-start = (bf16[512,512]{1,0:T(8,128)(2,1)S(1)}, bf16[512,512]{1,0:T(8,128)(2,1)}, u32[]{:S(2)}) copy-start(bf16[512,512]{1,0:T(8,128)(2,1)} %param.13) | copy-start | bytes 1572868
  8.7 1.5 copy-start.2
  10.2 55.7 %all-to-all-start.1 = ((bf16[1,32,8,4096]{3,1,0,2:T(8,128)(2,1)}), bf16[1,32,8,4096]{3,1,0,2:T(8,128)(2,1)}, u32[]{:S(2)}, u32[]{:S(2)}) async-start(bf16[1,32,8,4096]{3,1,0,2:T(8,128)(2,1)} %broadcast_multiply_fusion), calls=%async_computation.1 | async-start | bytes 4194304 | tf_op jit(solution)/shard_map/all_to_all | solution.py:82
  17.5 125.7 %all-gather.2.cloned.1.call-start = ((), (), s32[]{:S(2)}) async-start(), calls=%async_computation.4 | async-start | bytes 1310720 | tf_op jit(solution)/shard_map/all_gather | solution.py:105
  80.3 11.0 %collective-permute-start.1 = (bf16[1,1,32,1,2048]{4,0,2,3,1:T(2,128)(2,1)S(1)}, bf16[1,1,32,1,2048]{4,0,2,3,1:T(2,128)(2,1)S(1)}, u32[]{:S(2)}, u32[]{:S(2)}) collective-permute-start(bf16[1,1,32,1,2048]{4,0,2,3,1:T(2,128)(2,1)S(1)} %get-tuple-element.12), channel_id=1, source_target_pairs={{0,8},{4,12},{8,16},{12,20},{16,24},{20,28},{24,0},{28,4},{1,9},{5... | collective-permute-start | bytes 393224 | tf_op jit(solution)/shard_map/ppermute | solution.py:27
  80.3 21.2 %collective-permute-start = (bf16[1,1,32,1,2048]{4,0,2,3,1:T(2,128)(2,1)S(1)}, bf16[1,1,32,1,2048]{4,0,2,3,1:T(2,128)(2,1)S(1)}, u32[]{:S(2)}, u32[]{:S(2)}) collective-permute-start(bf16[1,1,32,1,2048]{4,0,2,3,1:T(2,128)(2,1)S(1)} %get-tuple-element.13), channel_id=1, source_target_pairs={{0,4},{4,8},{8,12},{12,16},{16,20},{20,24},{24,28},{28,0},{1,5},{5... | collective-permute-start | bytes 393224 | tf_op jit(solution)/shard_map/ppermute | solution.py:27
  81.8 94.6 %all-reduce.2.cloned.1.call-start = ((), (), s32[]{:S(2)}) async-start(), calls=%async_computation.5 | async-start | bytes 2097152 | tf_op jit(solution)/shard_map/psum | solution.py:92
  81.9 55.8 %collective-permute-start.6 = (bf16[1,1,32,1,2048]{4,0,2,3,1:T(2,128)(2,1)}, bf16[1,1,32,1,2048]{4,0,2,3,1:T(2,128)(2,1)S(1)}, u32[]{:S(2)}, u32[]{:S(2)}) collective-permute-start(bf16[1,1,32,1,2048]{4,0,2,3,1:T(2,128)(2,1)} %get-tuple-element.7), channel_id=1, source_target_pairs={{0,28},{4,0},{8,4},{12,8},{16,12},{20,16},{24,20},{28,24},{1,29},{... | collective-permute-start | bytes 393224 | tf_op jit(solution)/shard_map/ppermute | solution.py:27
  85.2 50.4 %collective-permute-start.5 = (bf16[1,1,32,1,2048]{4,0,2,3,1:T(2,128)(2,1)}, bf16[1,1,32,1,2048]{4,0,2,3,1:T(2,128)(2,1)S(1)}, u32[]{:S(2)}, u32[]{:S(2)}) collective-permute-start(bf16[1,1,32,1,2048]{4,0,2,3,1:T(2,128)(2,1)} %get-tuple-element.8), channel_id=1, source_target_pairs={{0,24},{4,28},{8,0},{12,4},{16,8},{20,12},{24,16},{28,20},{1,25},{... | collective-permute-start | bytes 393224 | tf_op jit(solution)/shard_map/ppermute | solution.py:27
  87.3 46.4 %collective-permute-start.4 = (bf16[1,1,32,1,2048]{4,0,2,3,1:T(2,128)(2,1)}, bf16[1,1,32,1,2048]{4,0,2,3,1:T(2,128)(2,1)S(1)}, u32[]{:S(2)}, u32[]{:S(2)}) collective-permute-start(bf16[1,1,32,1,2048]{4,0,2,3,1:T(2,128)(2,1)} %get-tuple-element.9), channel_id=1, source_target_pairs={{0,20},{4,24},{8,28},{12,0},{16,4},{20,8},{24,12},{28,16},{1,21},{... | collective-permute-start | bytes 393224 | tf_op jit(solution)/shard_map/ppermute | solution.py:27
  91.2 40.4 %collective-permute-start.3 = (bf16[1,1,32,1,2048]{4,0,2,3,1:T(2,128)(2,1)}, bf16[1,1,32,1,2048]{4,0,2,3,1:T(2,128)(2,1)S(1)}, u32[]{:S(2)}, u32[]{:S(2)}) collective-permute-start(bf16[1,1,32,1,2048]{4,0,2,3,1:T(2,128)(2,1)} %get-tuple-element.10), channel_id=1, source_target_pairs={{0,16},{4,20},{8,24},{12,28},{16,0},{20,4},{24,8},{28,12},{1,17},{... | collective-permute-start | bytes 393224 | tf_op jit(solution)/shard_map/ppermute | solution.py:27
  101.5 28.1 %collective-permute-start.2 = (bf16[1,1,32,1,2048]{4,0,2,3,1:T(2,128)(2,1)}, bf16[1,1,32,1,2048]{4,0,2,3,1:T(2,128)(2,1)S(1)}, u32[]{:S(2)}, u32[]{:S(2)}) collective-permute-start(bf16[1,1,32,1,2048]{4,0,2,3,1:T(2,128)(2,1)} %get-tuple-element.11), channel_id=1, source_target_pairs={{0,12},{4,16},{8,20},{12,24},{16,28},{20,0},{24,4},{28,8},{1,13},{... | collective-permute-start | bytes 393224 | tf_op jit(solution)/shard_map/ppermute | solution.py:27
  141.2 1.2 copy-start.3
  141.2 1.2 copy-start.6
  145.1 31.3 %copy-start.4 = (f32[16384]{0:T(1024)S(1)}, f32[16384]{0:T(1024)}, u32[]{:S(2)}) copy-start(f32[16384]{0:T(1024)} %param.16) | copy-start | bytes 196612
  146.6 35.1 %all-to-all-start = ((bf16[1,32,8,2048]{3,1,0,2:T(8,128)(2,1)}), bf16[1,32,8,2048]{3,1,0,2:T(8,128)(2,1)}, u32[]{:S(2)}, u32[]{:S(2)}) async-start(bf16[1,32,8,2048]{3,1,0,2:T(8,128)(2,1)} %copy.19), calls=%async_computation | async-start | bytes 2097152 | tf_op jit(solution)/shard_map/all_to_all | solution.py:107
  183.3 5.9 %copy-start.5 = (s32[4,16]{1,0:T(4,128)S(1)}, s32[4,16]{1,0:T(4,128)}, u32[]{:S(2)}) copy-start(s32[4,16]{1,0:T(4,128)} %param.19) | copy-start | bytes 772
  183.3 53.1 %all-to-all-start.2 = ((bf16[1,32,8,4096]{3,1,0,2:T(8,128)(2,1)}), bf16[1,32,8,4096]{3,1,0,2:T(8,128)(2,1)S(1)}, u32[]{:S(2)}, u32[]{:S(2)}) async-start(bf16[1,32,8,4096]{3,1,0,2:T(8,128)(2,1)} %broadcast_in_dim.49), calls=%async_computation.2 | async-start | bytes 4194304 | tf_op jit(solution)/shard_map/all_to_all | solution.py:114
  189.0 126.2 %reduce-scatter.2.cloned.1.call-start = ((), (), s32[]{:S(2)}) async-start(), calls=%async_computation.6 | async-start | bytes 5242880 | tf_op jit(solution)/shard_map/reduce_scatter | solution.py:129
  271.6 43.6 %copy-start.1 = (bf16[512,512]{1,0:T(8,128)(2,1)S(1)}, bf16[512,512]{1,0:T(8,128)(2,1)}, u32[]{:S(2)}) copy-start(bf16[512,512]{1,0:T(8,128)(2,1)} %param.13) | copy-start | bytes 1572868
Sparse Core Ops, SparseCore 0:
  81.9 17.1 all-gather.1
  142.5 33.8 all-reduce.1
  271.7 43.4 reduce-scatter.1
